TPU v7x, 32 devices: a whole 2x2x4 slice. The times are simulated.
32 devices in a mesh: row: 4 (over x, core), vec: 8 (over z, y).
Axes of the slice: x: 2, y: 2, z: 4, core: 2. Of those that a mesh axis runs over, the one named last changes fastest.
Arguments:
- old_vectors: float32 [640, 12288], P('vec', 'row'), may hold values from -6 to 6
- panel_source: int32 [256], replicated, may hold values from 0 to 639, as said below
- secular: float32 [1024, 256], P('vec'), may hold values from -0.375 to 0.375
- reflectors: float32 [256, 12288], P('vec', 'row'), may hold values from -6 to 6
- wy_factor: float32 [256, 256], replicated, as said below
- cholesky_panel: float32 [256, 12288], P('vec', 'row'), may hold values from -0.0546875 to 0.0546875
- panel_inverse: float32 [256, 256], replicated, as said below
Outputs:
- vectors: float32 [1024, 12288], P('vec', 'row')
Inputs may be any that keep to these rules, and one draw needn't show every extreme that they name: `panel_source`: distinct numbers; each block of 80 consecutive old vectors (those of one index of vec) supplies at most 48 panel columns, and some block supplies exactly 48. `wy_factor`: upper triangular. `panel_inverse`: upper triangular.
All inputs are finite; a program needn't handle non-finite values.
Results may differ from a plain program's by a relative error of at most 0.0001.
Values sent between devices are 32-bit elements; how exact they have to be, the bound alone decides.
A program may use at most 64 MiB of HBM per device.

v0:
```python
import jax
import jax.numpy as jnp
from jax import lax
from jax.sharding import PartitionSpec as P


def product(left, right):
    return jnp.dot(left, right, precision=lax.Precision.HIGHEST, preferred_element_type=jnp.float32)


def per_device(
    old_vectors, panel_source, secular, reflectors, wy_factor, cholesky_panel, panel_inverse
):
    panel_width = secular.shape[1]
    old_count = old_vectors.shape[0]
    row_count = old_vectors.shape[1]
    vec_width = lax.axis_size("vec")
    vec_index = lax.axis_index("vec")
    slots = 3 * (panel_width // vec_width) // 2
    owner_index = panel_source // old_count
    local_index = panel_source % old_count
    onehot = (owner_index[:, None] == jnp.arange(vec_width, dtype=jnp.int32)[None, :]).astype(
        jnp.int32
    )
    earlier = jnp.sum((jnp.cumsum(onehot, axis=0) - onehot) * onehot, axis=1)
    slot_index = owner_index * slots + earlier
    is_mine = owner_index == vec_index
    picker = (
        (earlier[:, None] == jnp.arange(slots, dtype=jnp.int32)[None, :]) & is_mine[:, None]
    ).astype(jnp.float32)
    localhot = (local_index[:, None] == jnp.arange(old_count, dtype=jnp.int32)[None, :]).astype(
        jnp.float32
    )
    chooser = product(picker.T, localhot)
    buffer = product(chooser, old_vectors)
    selector = (
        slot_index[:, None] == jnp.arange(slots * vec_width, dtype=jnp.int32)[None, :]
    ).astype(jnp.float32)
    mapped = product(secular, selector)
    gathered = product(mapped, lax.all_gather(buffer, "vec", axis=0, tiled=True))
    full_reflectors = lax.all_gather(reflectors, "vec", axis=0, tiled=True)
    full_cholesky = lax.all_gather(cholesky_panel, "vec", axis=0, tiled=True)
    row_index = lax.axis_index("row")
    global_rows = row_index * row_count + jnp.arange(row_count, dtype=jnp.int32)
    below_mask = jnp.where(global_rows >= panel_width, 1.0, 0.0).astype(jnp.float32)
    masked = full_cholesky * below_mask[None, :]
    inner_products = lax.psum(product(gathered, full_reflectors.T), "row")
    wy_coeff = product(inner_products, wy_factor.T)
    applied = gathered - product(wy_coeff, full_reflectors)
    correction = lax.psum(product(applied, masked.T), "row")
    head_rows = applied[:, :panel_width]
    solved = product(head_rows - correction, panel_inverse.T)
    top_rows = jnp.where(row_index == 0, solved, head_rows)
    return jnp.concatenate([top_rows, applied[:, panel_width:]], axis=1)


def solution(mesh):
    in_specs = (P("vec", "row"), P(), P("vec", None), P("vec", "row"), P(), P("vec", "row"), P())
    out_specs = P("vec", "row")
    return jax.shard_map(
        per_device, mesh=mesh, in_specs=in_specs, out_specs=out_specs, check_vma=False
    )
```

profile of v0, /device:TPU:0, one launch (start us, length us, event | category | flops | bytes accessed | tf_op | source)
XLA Modules:
  0.0 298.9 jit_solution(6794034859329231396)
XLA Ops:
  6.5 0.0 copy-start
  6.5 0.0 copy-start.4
  6.5 0.0 all-gather.4.cloned.1.call-start
  6.5 0.8 and_select_fusion
  7.3 0.7 broadcast_compare_fusion
  8.0 0.6 reduce-window.6
  8.6 0.2 slice_reduce_fusion
  8.9 0.1 fusion.17
  9.0 0.3 fusion.10
  9.3 0.0 copy-done
  9.3 1.5 fusion.19
  10.8 0.0 all-gather.4.cloned.1.call-update
  10.8 0.0 all-gather.6.cloned.1.call-start
  10.8 0.7 all-gather.6.cloned.1.call-update
  11.5 0.0 all-reduce.3.cloned.1.call-start
  11.6 0.0 copy-done.4
  11.6 0.4 fusion.4
  12.1 80.9 %all-gather.4.cloned.1.call-done = f32[384,3072]{1,0:T(8,128)} async-done(((f32[48,3072]{1,0:T(8,128)}), f32[384,3072]{1,0:T(8,128)}) %all-gather.4.cloned.1.call-update) | async-done | bytes 4718608 | tf_op jit(solution)/shard_map/all_gather | solution.py:40
  93.0 4.8 %fusion.20 = f32[128,3072]{1,0:T(8,128)S(1)} fusion(f32[384,128]{1,0:T(8,128)S(1)} %fusion.4, f32[384,3072]{1,0:T(8,128)} %all-gather.4.cloned.1.call-done), kind=kOutput, calls=%fused_computation.34 | convolution fusion | flops 1811939328 | bytes 6488064 | tf_op jit(solution)/shard_map/dot_general | solution.py:8
  97.8 0.0 copy-start.1
  97.8 0.0 copy-start.2
  97.9 55.7 %all-gather.6.cloned.1.call-done = f32[256,3072]{1,0:T(8,128)} async-done(((f32[32,3072]{1,0:T(8,128)}), f32[256,3072]{1,0:T(8,128)}) %all-gather.6.cloned.1.call-update) | async-done | bytes 3145744 | tf_op jit(solution)/shard_map/all_gather | solution.py:41
  153.6 5.8 %fusion.21 = f32[128,256]{1,0:T(8,128)} fusion(f32[128,3072]{1,0:T(8,128)S(1)} %fusion.20, f32[256,3072]{1,0:T(8,128)} %all-gather.6.cloned.1.call-done), kind=kOutput, calls=%fused_computation.35 | convolution fusion | flops 1207959552 | bytes 4849664 | tf_op jit(solution)/shard_map/dot_general | solution.py:8
  159.4 0.0 copy-done.1
  159.4 0.0 all-reduce.3.cloned.1.call-update
  159.4 0.0 all-gather.8.cloned.1.call-start
  159.5 0.5 all-gather.8.cloned.1.call-update
  160.0 0.0 all-reduce.5.cloned.1.call-start
  160.0 30.0 %all-reduce.3.cloned.1.call-done = f32[128,256]{1,0:T(8,128)} async-done(((f32[128,256]{1,0:T(8,128)}), f32[128,256]{1,0:T(8,128)}) %all-reduce.3.cloned.1.call-update) | async-done | bytes 131088 | tf_op jit(solution)/shard_map/psum | solution.py:47
  190.0 0.0 copy-done.2
  190.0 1.3 fusion.22
  191.3 4.1 %convolution_subtract_fusion = f32[128,3072]{1,0:T(8,128)S(1)} fusion(f32[128,3072]{1,0:T(8,128)} %copy-done.1, f32[128,256]{1,0:T(8,128)S(1)} %fusion.22, f32[256,3072]{1,0:T(8,128)} %all-gather.6.cloned.1.call-done), kind=kOutput, calls=%fused_computation | convolution fusion | flops 1208352768 | bytes 6422528 | tf_op jit(solution)/shard_map/dot_general | solution.py:8
  195.4 56.7 %all-gather.8.cloned.1.call-done = f32[256,3072]{1,0:T(8,128)} async-done(((f32[32,3072]{1,0:T(8,128)}), f32[256,3072]{1,0:T(8,128)}) %all-gather.8.cloned.1.call-update) | async-done | bytes 3145744 | tf_op jit(solution)/shard_map/all_gather | solution.py:42
  252.1 5.7 %fusion = f32[128,256]{1,0:T(8,128)} fusion(f32[128,3072]{1,0:T(8,128)S(1)} %convolution_subtract_fusion, f32[256,3072]{1,0:T(8,128)} %all-gather.8.cloned.1.call-done, f32[3072]{0:T(1024)S(1)} %fusion.15), kind=kOutput, calls=%fused_computation.1 | convolution fusion | flops 1208745984 | bytes 4861952 | tf_op jit(solution)/shard_map/dot_general | solution.py:8
  257.8 0.0 copy-start.3
  257.8 0.0 all-reduce.5.cloned.1.call-update
  257.9 1.2 slice.18
  259.1 29.3 %all-reduce.5.cloned.1.call-done = f32[128,256]{1,0:T(8,128)} async-done(((f32[128,256]{1,0:T(8,128)}), f32[128,256]{1,0:T(8,128)}) %all-reduce.5.cloned.1.call-update) | async-done | bytes 131088 | tf_op jit(solution)/shard_map/psum | solution.py:50
  288.4 0.0 copy-done.3
  288.4 1.3 convolution_select_fusion
  289.8 2.7 pad_maximum_fusion
  (5 shorter events, 0.1 us)
Async XLA Ops:
  6.5 2.8 copy-start
  6.5 5.1 %copy-start.4 = (f32[128,256]{1,0:T(8,128)S(1)}, f32[128,256]{1,0:T(8,128)}, u32[]{:S(2)}) copy-start(f32[128,256]{1,0:T(8,128)} %param.9) | copy-start | bytes 393220
  6.5 86.5 %all-gather.4.cloned.1.call-start = ((), (), s32[]{:S(2)}) async-start(), calls=%async_computation | async-start | bytes 5308416 | tf_op jit(solution)/shard_map/all_gather | solution.py:40
  10.8 142.8 %all-gather.6.cloned.1.call-start = ((), (), s32[]{:S(2)}) async-start(), calls=%async_computation.1 | async-start | bytes 3538944 | tf_op jit(solution)/shard_map/all_gather | solution.py:41
  11.5 178.5 %all-reduce.3.cloned.1.call-start = ((), (), s32[]{:S(2)}) async-start(), calls=%async_computation.2 | async-start | bytes 262144 | tf_op jit(solution)/shard_map/psum | solution.py:47
  97.8 61.5 %copy-start.1 = (f32[128,3072]{1,0:T(8,128)}, f32[128,3072]{1,0:T(8,128)S(1)}, u32[]{:S(2)}) copy-start(f32[128,3072]{1,0:T(8,128)S(1)} %fusion.20) | copy-start | bytes 4718596
  97.8 92.2 %copy-start.2 = (f32[256,256]{1,0:T(8,128)S(1)}, f32[256,256]{1,0:T(8,128)}, u32[]{:S(2)}) copy-start(f32[256,256]{1,0:T(8,128)} %param.11) | copy-start | bytes 786436
  159.4 92.7 %all-gather.8.cloned.1.call-start = ((), (), s32[]{:S(2)}) async-start(), calls=%async_computation.3 | async-start | bytes 3538944 | tf_op jit(solution)/shard_map/all_gather | solution.py:42
  160.0 128.5 %all-reduce.5.cloned.1.call-start = ((), (), s32[]{:S(2)}) async-start(), calls=%async_computation.4 | async-start | bytes 262144 | tf_op jit(solution)/shard_map/psum | solution.py:50
  257.8 30.6 %copy-start.3 = (f32[256,256]{1,0:T(8,128)S(1)}, f32[256,256]{1,0:T(8,128)}, u32[]{:S(2)}) copy-start(f32[256,256]{1,0:T(8,128)} %param.13) | copy-start | bytes 786436
Sparse Core Ops, SparseCore 0:
  10.9 82.0 all-gather.3
  95.2 58.3 all-gather.5
  159.5 30.4 all-reduce.2
  192.0 60.0 all-gather.7
  258.0 30.4 all-reduce.4
where the time goes:
time: 299 us
  waiting for transfers between devices  254 us (85%)
  matrix products  25.3 us (8%)
  between operations  13.3 us (4%)
  other arithmetic  4.86 us (2%)
    all_gather x1, waiting for transfers between devices, per_device(): lax.all_gather(buffer, 'vec', axis=0, tiled=True)  80.9 us
    all_gather x1, waiting for transfers between devices, per_device(): full_cholesky = lax.all_gather(cholesky_panel, 'vec', axis=0, tiled=True)  56.7 us
    all_gather x1, waiting for transfers between devices, per_device(): full_reflectors = lax.all_gather(reflectors, 'vec', axis=0, tiled=True)  55.7 us
    psum x1, waiting for transfers between devices, per_device(): inner_products = lax.psum(product(gathered, full_reflectors.T), 'row')  30 us
    psum x1, waiting for transfers between devices, per_device(): correction = lax.psum(product(applied, masked.T), 'row')  29.3 us
    dot_general x9, matrix products, product(): jnp.dot(left, right, precision=lax.Precision.HIGHEST, preferred_element_t...  25.3 us
  transfers between devices with their start and end apart: 5, of which 5 were waited for; matrix products, arithmetic and copies ran while one was open for 4% of the time, Pallas kernels for 0%

commit v1 on v0

v1 whole, which is shorter than its diff:
```python
import functools
import math

import jax
import jax.numpy as jnp
from jax import lax
from jax.experimental import pallas as pl
from jax.experimental.pallas import tpu as pltpu
from jax.sharding import PartitionSpec as P

MESH = pl.DeviceIdType.MESH


def product(left, right):
    return jnp.dot(left, right, precision=lax.Precision.HIGHEST, preferred_element_type=jnp.float32)


def product_t(left, right):
    return lax.dot_general(
        left,
        right,
        (((1,), (1,)), ((), ())),
        precision=lax.Precision.HIGHEST,
        preferred_element_type=jnp.float32,
    )


def kernel(
    nrow, zn, yn, slots,
    own_ref, chol_ref, slot_ref, secular_ref, wy_ref, pinv_ref,
    out_ref,
    kbuf, gram, rbuf, gall_y, gall_c, smap,
    own_sem, send_z, send_y, recv_k, send_r, recv_r, send_g, recv_g, send_c, recv_c,
):
    nvec = zn * yn
    rows, ncol = own_ref.shape
    refl = rows - slots
    panel = secular_ref.shape[1]
    r = lax.axis_index("row")
    v = lax.axis_index("vec")
    z = v // yn
    y = v % yn

    barrier = pltpu.get_barrier_semaphore()

    @pl.loop(1, nrow)
    def _(k):
        pl.semaphore_signal(barrier, inc=1, device_id=((r + k) % nrow, v), device_id_type=MESH)

    @pl.loop(1, nvec)
    def _(k):
        pl.semaphore_signal(barrier, inc=1, device_id=(r, (v + k) % nvec), device_id_type=MESH)

    pl.semaphore_wait(barrier, nrow - 1 + nvec - 1)

    def block_copy(src, block, target, send_sem):
        return pltpu.make_async_remote_copy(
            src_ref=src,
            dst_ref=kbuf.at[block],
            send_sem=send_sem,
            recv_sem=recv_k.at[block],
            device_id=(r, target),
            device_id_type=MESH,
        )

    def z_copy(src, block, sign):
        return block_copy(src, block, v + sign * yn, send_z.at[(sign + 1) // 2, block])

    def y_copy(src, block, sign):
        return block_copy(src, block, v + sign, send_y.at[(sign + 1) // 2, block])

    def z_ok(sign):
        return (z + sign >= 0) & (z + sign < zn)

    def y_ok(sign):
        return (y + sign >= 0) & (y + sign < yn)

    own_copy = pltpu.make_async_copy(own_ref, kbuf.at[v], own_sem)
    for sign in (-1, 1):

        @pl.when(z_ok(sign))
        def _():
            z_copy(own_ref, v, sign).start()

        @pl.when(y_ok(sign))
        def _():
            y_copy(own_ref, v, sign).start()

    own_copy.start()
    gram[...] = jnp.zeros_like(gram)
    row_iota = lax.broadcasted_iota(jnp.int32, (nvec * slots, panel), 0)
    every = jnp.where(row_iota == slot_ref[0:1, :], 1.0, 0.0).astype(jnp.float32)
    smap[...] = product_t(secular_ref[...], every)

    step = math.gcd(ncol, 768)

    def add_gram(block):
        def body(i, carry):
            with_y, with_c, y_with_c = carry
            cols = pl.ds(pl.multiple_of(i * step, step), step)
            picked = kbuf[block, 0:slots, cols]
            with_y = with_y + product_t(own_ref[slots:rows, cols], picked)
            masked = chol_ref[:, cols]
            with_c = with_c + product_t(masked, picked)
            y_with_c = y_with_c + product_t(masked, kbuf[block, slots:rows, cols])
            return with_y, with_c, y_with_c

        zero = jnp.zeros((refl, slots), jnp.float32)
        with_y, with_c, y_with_c = lax.fori_loop(
            0, ncol // step, body, (zero, zero, jnp.zeros((refl, refl), jnp.float32))
        )
        slot_iota = lax.broadcasted_iota(jnp.int32, (slots, panel), 0) + block * slots
        chosen = jnp.where(slot_iota == slot_ref[0:1, :], 1.0, 0.0).astype(jnp.float32)
        lane = lax.broadcasted_iota(jnp.int32, (refl, panel), 1)
        sub = lax.broadcasted_iota(jnp.int32, (refl, panel), 0) + block * refl
        placed = jnp.where(lane == sub, 1.0, 0.0).astype(jnp.float32)
        gram[0:refl] += product(with_y, chosen)
        gram[refl : 2 * refl] += product(with_c, chosen)
        gram[2 * refl : 3 * refl] += product(y_with_c, placed)

    own_copy.wait()
    add_gram(v)

    def wait_block(block):
        pltpu.make_async_remote_copy(
            src_ref=kbuf.at[block],
            dst_ref=kbuf.at[block],
            send_sem=own_sem,
            recv_sem=recv_k.at[block],
            device_id=(r, v),
            device_id_type=MESH,
        ).wait_recv()

    @pl.loop(1, zn + 1)
    def _(d):
        for side in (-1, 1):
            zz = z + side * d

            @pl.when((zz >= 0) & (zz < zn))
            def _():
                block = zz * yn + y
                wait_block(block)

                @pl.when(z_ok(-side))
                def _():
                    z_copy(kbuf.at[block], block, -side).start()

                for sign in (-1, 1):

                    @pl.when(y_ok(sign))
                    def _():
                        y_copy(kbuf.at[block], block, sign).start()

        for side in (-1, 1):
            zz = z + side * d

            @pl.when((zz >= 0) & (zz < zn))
            def _():
                add_gram(zz * yn + y)

        e = d - 1
        for side in (-1, 1):
            zz = z + side * e

            @pl.when((zz >= 0) & (zz < zn) & ((side < 0) | (e > 0)))
            def _():
                @pl.loop(1, yn)
                def _(h):
                    for sign in (-1, 1):
                        yy = y + sign * h

                        @pl.when((yy >= 0) & (yy < yn))
                        def _():
                            block = zz * yn + yy
                            wait_block(block)

                            @pl.when(y_ok(-sign))
                            def _():
                                y_copy(kbuf.at[block], block, -sign).start()

                            add_gram(block)

    rbuf[r] = gram[...]

    def row_copy(k):
        return pltpu.make_async_remote_copy(
            src_ref=gram,
            dst_ref=rbuf.at[r],
            send_sem=send_r.at[k],
            recv_sem=recv_r.at[r],
            device_id=((r + k) % nrow, v),
            device_id_type=MESH,
        )

    def row_arrival(k):
        return pltpu.make_async_remote_copy(
            src_ref=gram,
            dst_ref=rbuf.at[(r + k) % nrow],
            send_sem=send_r.at[k],
            recv_sem=recv_r.at[(r + k) % nrow],
            device_id=((r + k) % nrow, v),
            device_id_type=MESH,
        )

    @pl.loop(1, nrow)
    def _(k):
        row_copy(k).start()

    wide = math.gcd(ncol, 512)

    def merge(low, high):
        @pl.loop(low, high)
        def _(i):
            cols = pl.ds(pl.multiple_of(i * wide, wide), wide)
            picked = kbuf[:, 0:slots, cols].reshape(nvec * slots, wide)
            out_ref[:, cols] = product(smap[...], picked)

    half = (ncol // wide) // 2
    merge(0, half)

    @pl.loop(1, nrow)
    def _(k):
        row_arrival(k).wait_recv()

    total = rbuf[0]
    for k in range(1, nrow):
        total = total + rbuf[k]
    gall_y[v] = total[0:refl]
    gall_c[v] = total[refl:]

    def vec_copy(buf, send, recv, k, slot):
        return pltpu.make_async_remote_copy(
            src_ref=buf.at[v],
            dst_ref=buf.at[slot],
            send_sem=send.at[k],
            recv_sem=recv.at[slot],
            device_id=(r, (v + k) % nvec),
            device_id_type=MESH,
        )

    @pl.loop(1, nvec)
    def _(k):
        vec_copy(gall_y, send_g, recv_g, k, v).start()

    @pl.when(r == 0)
    def _():
        @pl.loop(1, nvec)
        def _(k):
            vec_copy(gall_c, send_c, recv_c, k, v).start()

    merge(half, ncol // wide)

    @pl.loop(1, nvec)
    def _(k):
        vec_copy(gall_y, send_g, recv_g, k, (v + k) % nvec).wait_recv()

    inner = product_t(secular_ref[...], gall_y[...].reshape(panel, panel))
    coeff = product_t(inner, wy_ref[...])

    @pl.loop(0, ncol // wide)
    def _(i):
        cols = pl.ds(pl.multiple_of(i * wide, wide), wide)
        householder = kbuf[:, slots:rows, cols].reshape(panel, wide)
        out_ref[:, cols] = out_ref[:, cols] - product(coeff, householder)

    @pl.when(r == 0)
    def _():
        @pl.loop(1, nvec)
        def _(k):
            vec_copy(gall_c, send_c, recv_c, k, (v + k) % nvec).wait_recv()

        with_c = gall_c[:, 0:refl].reshape(panel, panel)
        y_with_c = gall_c[:, refl : 2 * refl].reshape(panel, panel)
        correction = product_t(secular_ref[...], with_c) - product_t(coeff, y_with_c)
        out_ref[:, 0:panel] = product_t(out_ref[:, 0:panel] - correction, pinv_ref[...])

        @pl.loop(1, nvec)
        def _(k):
            vec_copy(gall_c, send_c, recv_c, k, v).wait_send()

    @pl.loop(1, nvec)
    def _(k):
        vec_copy(gall_y, send_g, recv_g, k, v).wait_send()

    @pl.loop(1, nrow)
    def _(k):
        row_copy(k).wait_send()

    @pl.loop(0, zn)
    def _(zz):
        block = zz * yn + y
        for sign in (-1, 1):
            passes = zz <= z if sign > 0 else zz >= z

            @pl.when(z_ok(sign) & passes)
            def _():
                z_copy(kbuf.at[block], block, sign).wait_send()

        @pl.loop(0, yn)
        def _(yy):
            other = zz * yn + yy
            for sign in (-1, 1):
                passes = yy <= y if sign > 0 else yy >= y

                @pl.when(y_ok(sign) & passes)
                def _():
                    y_copy(kbuf.at[other], other, sign).wait_send()


def per_device(
    nrow, nvec,
    old_vectors, panel_source, secular, reflectors, wy_factor, cholesky_panel, panel_inverse,
):
    panel = secular.shape[1]
    old_count, ncol = old_vectors.shape
    refl = reflectors.shape[0]
    yn = max(1, math.isqrt(nvec // 2))
    zn = nvec // yn
    slots = -(-(3 * (panel // nvec) // 2) // 8) * 8
    v = lax.axis_index("vec")
    r = lax.axis_index("row")
    owner = panel_source // old_count
    local = panel_source % old_count
    order = jnp.arange(panel, dtype=jnp.int32)
    before = (owner[:, None] == owner[None, :]) & (order[None, :] < order[:, None])
    earlier = jnp.sum(before.astype(jnp.int32), axis=1)
    slot_index = owner * slots + earlier
    mine = jnp.where(owner == v, earlier, -1)
    hit = mine[None, :] == jnp.arange(slots, dtype=jnp.int32)[:, None]
    source = jnp.sum(jnp.where(hit, local[None, :] + 1, 0), axis=1) - 1
    chooser = (source[:, None] == jnp.arange(old_count, dtype=jnp.int32)[None, :]).astype(
        jnp.float32
    )
    own = jnp.concatenate([product(chooser, old_vectors), reflectors], axis=0)
    below = r * ncol + jnp.arange(ncol, dtype=jnp.int32) >= panel
    masked = jnp.where(below[None, :], cholesky_panel, 0.0)
    rows = slots + refl
    vmem = pl.BlockSpec(memory_space=pltpu.VMEM)
    dma = pltpu.SemaphoreType.DMA
    return pl.pallas_call(
        functools.partial(kernel, nrow, zn, yn, slots),
        out_shape=jax.ShapeDtypeStruct((secular.shape[0], ncol), jnp.float32),
        in_specs=[vmem] * 6,
        out_specs=vmem,
        scratch_shapes=[
            pltpu.VMEM((nvec, rows, ncol), jnp.float32),
            pltpu.VMEM((3 * refl, panel), jnp.float32),
            pltpu.VMEM((nrow, 3 * refl, panel), jnp.float32),
            pltpu.VMEM((nvec, refl, panel), jnp.float32),
            pltpu.VMEM((nvec, 2 * refl, panel), jnp.float32),
            pltpu.VMEM((secular.shape[0], nvec * slots), jnp.float32),
            dma,
            dma((2, nvec)),
            dma((2, nvec)),
            dma((nvec,)),
            dma((nrow,)),
            dma((nrow,)),
            dma((nvec,)),
            dma((nvec,)),
            dma((nvec,)),
            dma((nvec,)),
        ],
        compiler_params=pltpu.CompilerParams(
            collective_id=0, has_side_effects=True, vmem_limit_bytes=48 * 1024 * 1024
        ),
    )(own, masked, slot_index[None, :], secular, wy_factor, panel_inverse)


def solution(mesh):
    in_specs = (P("vec", "row"), P(), P("vec", None), P("vec", "row"), P(), P("vec", "row"), P())
    return jax.shard_map(
        functools.partial(per_device, mesh.shape["row"], mesh.shape["vec"]),
        mesh=mesh,
        in_specs=in_specs,
        out_specs=P("vec", "row"),
        check_vma=False,
    )
```

time: 299 us -> 118 us (0.39)
  waiting for transfers between devices: 254 us -> 0 us
  Pallas kernels: 0 us -> 113 us
  matrix products: 25.3 us -> 0.54 us
  between operations: 13.3 us -> 0.09 us
    all_gather x3 -> x0, waiting for transfers between devices: 193 us -> none  [the longest x1 80.9 us: per_device(): lax.all_gather(buffer, 'vec', axis=0, tiled=True)]
    pallas_call x0 -> x1, Pallas kernels: none -> 113 us  [per_device(): pl.pallas_call(functools.partial(kernel, nrow, zn, yn, slots), out_shape=...]
    psum x2 -> x0, waiting for transfers between devices: 59.3 us -> none  [the longest x1 30 us: per_device(): inner_products = lax.psum(product(gathered, full_reflectors.T), 'row')]
    dot_general x9 -> x1, matrix products: 25.3 us -> 0.54 us  [product(): jnp.dot(left, right, precision=lax.Precision.HIGHEST, preferred_element_t...]
  transfers between devices with their start and end apart: 5 -> 0, of which waited for: 5 -> 0; matrix products, arithmetic and copies ran while one was open for 4% -> 0% of each run, Pallas kernels for 0% -> 0%
where the time goes in v1:
time: 118 us
  Pallas kernels  113 us (96%)
  other arithmetic  2.21 us (2%)
  local copies, waits for them, and re-layouts  1.56 us (1%)
    pallas_call x1, Pallas kernels, per_device(): pl.pallas_call(functools.partial(kernel, nrow, zn, yn, slots), out_shape=...  113 us

profile of v1, /device:TPU:0, one launch (start us, length us, event | category | flops | bytes accessed | tf_op | source)
XLA Modules:
  0.0 117.7 jit_solution(7994235937340017640)
XLA Ops:
  0.0 0.0 copy-start
  0.0 0.0 copy-start.4
  0.0 0.8 and_select_fusion.1
  0.8 0.2 convert_reduce_fusion
  1.0 0.1 select_reduce_fusion
  1.1 1.0 broadcast_select_fusion.chol_ref
  2.2 0.0 copy-done
  2.2 0.0 copy-start.1
  2.2 0.0 copy-start.2
  2.2 0.0 copy-start.3
  2.2 0.5 fusion.1
  2.8 0.0 copy-done.4
  2.8 0.1 pad_maximum_fusion.own_ref
  2.9 0.3 copy-done.1
  3.1 0.1 copy-done.2
  3.2 0.0 copy-done.3
  3.2 113.3 %shard_map.73 = f32[128,3072]{1,0:T(8,128)S(1)} custom-call(f32[80,3072]{1,0:T(8,128)S(1)} %pad_maximum_fusion.own_ref, f32[32,3072]{1,0:T(8,128)S(1)} %broadcast_select_fusion.chol_ref, s32[1,256]{1,0:T(1,128)S(1)} %bitcast.2, f32[128,256]{1,0:T(8,128)S(1)} %copy-done.3, f32[256,256]{1,0:T(8,128)S(1)} %copy-done.1, f32[256,256]{1,0:T(8,128)S(1)} %copy-done.2), custom_call_target="tpu_custom_call" | custom-call | tf_op jit(solution)/shard_map/pallas_call | solution.py:340
  116.5 1.1 copy.9
  (3 shorter events, 0.0 us)
Async XLA Ops:
  0.0 2.2 %copy-start = (f32[80,3072]{1,0:T(8,128)S(1)}, f32[80,3072]{1,0:T(8,128)}, u32[]{:S(2)}) copy-start(f32[80,3072]{1,0:T(8,128)} %param.7) | copy-start | bytes 2949124
  0.0 2.8 %copy-start.4 = (f32[32,3072]{1,0:T(8,128)S(1)}, f32[32,3072]{1,0:T(8,128)}, u32[]{:S(2)}) copy-start(f32[32,3072]{1,0:T(8,128)} %param.10) | copy-start | bytes 1179652
  2.2 1.0 copy-start.1
  2.2 1.0 copy-start.2
  2.2 1.0 copy-start.3

commit v2 on v1

v2 whole, which is shorter than its diff:
```python
import functools
import math

import jax
import jax.numpy as jnp
from jax import lax
from jax.experimental import pallas as pl
from jax.experimental.pallas import tpu as pltpu
from jax.sharding import PartitionSpec as P

MESH = pl.DeviceIdType.MESH


def product(left, right):
    return jnp.dot(left, right, precision=lax.Precision.HIGHEST, preferred_element_type=jnp.float32)


def product_t(left, right):
    return lax.dot_general(
        left,
        right,
        (((1,), (1,)), ((), ())),
        precision=lax.Precision.HIGHEST,
        preferred_element_type=jnp.float32,
    )


def kernel(
    nrow, zn, yn, slots,
    own_ref, chol_ref, slot_ref, secular_ref, wy_ref, pinv_ref,
    out_ref,
    kbuf, gram, gram_y, rbuf, rbuf_y, gall, smap,
    own_sem, send_k, recv_k, send_r, recv_r, send_ry, recv_ry, send_g, recv_g,
):
    nvec = zn * yn
    rows, ncol = own_ref.shape
    refl = rows - slots
    panel = secular_ref.shape[1]
    r = lax.axis_index("row")
    v = lax.axis_index("vec")
    z = v // yn
    y = v % yn
    share = (zn * (yn - 1) - (zn - 1)) / max(1, 2 * (zn - 1) * (yn - 1))
    late = min(max(round(share * ncol / 128), 1) * 128, ncol - 128)
    early = ncol - late

    barrier = pltpu.get_barrier_semaphore()

    @pl.loop(1, nrow)
    def _(k):
        pl.semaphore_signal(barrier, inc=1, device_id=((r + k) % nrow, v), device_id_type=MESH)

    @pl.loop(1, nvec)
    def _(k):
        pl.semaphore_signal(barrier, inc=1, device_id=(r, (v + k) % nvec), device_id_type=MESH)

    pl.semaphore_wait(barrier, nrow - 1 + nvec - 1)

    def z_ok(sign):
        return (z + sign >= 0) & (z + sign < zn)

    def y_ok(sign):
        return (y + sign >= 0) & (y + sign < yn)

    def part_copy(phase, part, block, target, lane, own):
        low, size = ((0, slots), (slots, refl))[phase]
        start, width = ((0, early), (early, late))[part]
        index = (pl.ds(low, size), pl.ds(start, width))
        held = kbuf.at[(block,) + index]
        return pltpu.make_async_remote_copy(
            src_ref=own_ref.at[index] if own else held,
            dst_ref=held,
            send_sem=send_k.at[phase, part, lane, block],
            recv_sem=recv_k.at[phase, part, block],
            device_id=(r, target),
            device_id_type=MESH,
        )

    def z_copy(phase, part, block, sign, own=False):
        return part_copy(phase, part, block, v + sign * yn, (sign + 1) // 2, own)

    def y_copy(phase, part, block, sign, own=False):
        return part_copy(phase, part, block, v + sign, 2 + (sign + 1) // 2, own)

    def z_send(phase, part, block, sign, own=False):
        @pl.when(z_ok(sign))
        def _():
            z_copy(phase, part, block, sign, own).start()

    def y_send(phase, part, block, sign, own=False):
        @pl.when(y_ok(sign))
        def _():
            y_copy(phase, part, block, sign, own).start()

    def arrived(phase, part, block):
        part_copy(phase, part, block, v, 0, False).wait_recv()

    def send_own(phase):
        for sign in (-1, 1):
            y_send(phase, 1, v, sign, True)
            z_send(phase, 0, v, sign, True)
        for sign in (-1, 1):
            y_send(phase, 0, v, sign, True)
            z_send(phase, 1, v, sign, True)

    def relay_first(phase):
        @pl.loop(1, yn)
        def _(h):
            for side in (-1, 1):
                yy = y + side * h

                @pl.when((yy >= 0) & (yy < yn))
                def _():
                    block = z * yn + yy
                    arrived(phase, 1, block)
                    y_send(phase, 1, block, -side)
                    for sign in (-1, 1):
                        z_send(phase, 1, block, sign)

    def relay(phase, use, hook):
        @pl.loop(1, zn + 1)
        def _(d):
            for side in (-1, 1):
                zz = z + side * d

                @pl.when((zz >= 0) & (zz < zn))
                def _():
                    block = zz * yn + y
                    arrived(phase, 0, block)
                    z_send(phase, 0, block, -side)
                    for sign in (-1, 1):
                        y_send(phase, 0, block, sign)

            for side in (-1, 1):
                zz = z + side * d

                @pl.when((zz >= 0) & (zz < zn))
                def _():
                    @pl.loop(0, yn)
                    def _(yy):
                        arrived(phase, 1, zz * yn + yy)
                        z_send(phase, 1, zz * yn + yy, -side)

            for side in (-1, 1):
                zz = z + side * d

                @pl.when((zz >= 0) & (zz < zn))
                def _():
                    use(zz * yn + y)

            e = d - 1
            for side in (-1, 1):
                zz = z + side * e

                @pl.when((zz >= 0) & (zz < zn) & ((side < 0) | (e > 0)))
                def _():
                    @pl.loop(1, yn)
                    def _(h):
                        for sign in (-1, 1):
                            yy = y + sign * h

                            @pl.when((yy >= 0) & (yy < yn))
                            def _():
                                block = zz * yn + yy
                                arrived(phase, 0, block)
                                y_send(phase, 0, block, -sign)
                                use(block)

            hook(d)

    own_copy = pltpu.make_async_copy(own_ref, kbuf.at[v], own_sem)
    send_own(0)
    own_copy.start()
    gram[...] = jnp.zeros_like(gram)
    gram_y[...] = jnp.zeros_like(gram_y)
    row_iota = lax.broadcasted_iota(jnp.int32, (nvec * slots, panel), 0)
    every = jnp.where(row_iota == slot_ref[0:1, :], 1.0, 0.0).astype(jnp.float32)
    smap[...] = product_t(secular_ref[...], every)

    step = math.gcd(ncol, 768)

    def add_picked(block):
        def body(i, carry):
            with_y, with_c = carry
            cols = pl.ds(pl.multiple_of(i * step, step), step)
            picked = kbuf[block, 0:slots, cols]
            with_y = with_y + product_t(own_ref[slots:rows, cols], picked)
            with_c = with_c + product_t(chol_ref[:, cols], picked)
            return with_y, with_c

        zero = jnp.zeros((refl, slots), jnp.float32)
        with_y, with_c = lax.fori_loop(0, ncol // step, body, (zero, zero))
        slot_iota = lax.broadcasted_iota(jnp.int32, (slots, panel), 0) + block * slots
        chosen = jnp.where(slot_iota == slot_ref[0:1, :], 1.0, 0.0).astype(jnp.float32)
        gram[0:refl] += product(with_y, chosen)
        gram[refl : 2 * refl] += product(with_c, chosen)

    def add_reflectors(block):
        def body(i, carry):
            cols = pl.ds(pl.multiple_of(i * step, step), step)
            return carry + product_t(chol_ref[:, cols], kbuf[block, slots:rows, cols])

        y_with_c = lax.fori_loop(0, ncol // step, body, jnp.zeros((refl, refl), jnp.float32))
        lane = lax.broadcasted_iota(jnp.int32, (refl, panel), 1)
        sub = lax.broadcasted_iota(jnp.int32, (refl, panel), 0) + block * refl
        placed = jnp.where(lane == sub, 1.0, 0.0).astype(jnp.float32)
        gram_y[...] += product(y_with_c, placed)

    own_copy.wait()
    relay_first(0)
    add_picked(v)
    relay(0, add_picked, lambda d: None)

    def row_copy(k, slot):
        return pltpu.make_async_remote_copy(
            src_ref=gram,
            dst_ref=rbuf.at[slot],
            send_sem=send_r.at[k],
            recv_sem=recv_r.at[slot],
            device_id=((r + k) % nrow, v),
            device_id_type=MESH,
        )

    def row_y_copy(slot):
        return pltpu.make_async_remote_copy(
            src_ref=gram_y,
            dst_ref=rbuf_y.at[slot],
            send_sem=send_ry,
            recv_sem=recv_ry.at[slot],
            device_id=(0, v),
            device_id_type=MESH,
        )

    def vec_copy(kind, k, slot):
        return pltpu.make_async_remote_copy(
            src_ref=gall.at[kind, v],
            dst_ref=gall.at[kind, slot],
            send_sem=send_g.at[kind, k],
            recv_sem=recv_g.at[kind, slot],
            device_id=(r, (v + k) % nvec),
            device_id_type=MESH,
        )

    def vec_start(kind):
        @pl.loop(1, nvec)
        def _(k):
            vec_copy(kind, k, v).start()

    def vec_arrive(kind):
        @pl.loop(1, nvec)
        def _(k):
            vec_copy(kind, k, (v + k) % nvec).wait_recv()

    def vec_sent(kind):
        @pl.loop(1, nvec)
        def _(k):
            vec_copy(kind, k, v).wait_send()

    wide = math.gcd(ncol, 512)

    def merge(low, high):
        @pl.loop(low, high)
        def _(i):
            cols = pl.ds(pl.multiple_of(i * wide, wide), wide)
            picked = kbuf[:, 0:slots, cols].reshape(nvec * slots, wide)
            out_ref[:, cols] = product(smap[...], picked)

    half = (ncol // wide) // 2

    @pl.loop(1, nrow)
    def _(k):
        row_copy(k, r).start()

    send_own(1)
    rbuf[r] = gram[...]
    relay_first(1)
    add_reflectors(v)

    def hook(d):
        @pl.when(d == 1)
        def _():
            @pl.loop(1, nrow)
            def _(k):
                row_copy(k, (r + k) % nrow).wait_recv()

            total = rbuf[0]
            for k in range(1, nrow):
                total = total + rbuf[k]
            gall[0, v] = total[0:refl]
            gall[1, v] = total[refl : 2 * refl]
            vec_start(0)

            @pl.when(r == 0)
            def _():
                vec_start(1)

            merge(0, half)

        @pl.when(d == 2)
        def _():
            merge(half, ncol // wide)

    relay(1, add_reflectors, hook)

    @pl.when(r != 0)
    def _():
        row_y_copy(r).start()

    vec_arrive(0)
    inner = product_t(secular_ref[...], gall[0].reshape(panel, panel))
    coeff = product_t(inner, wy_ref[...])

    @pl.when(r == 0)
    def _():
        total = gram_y[...]
        for k in range(1, nrow):
            row_y_copy(k).wait_recv()
            total = total + rbuf_y[k]
        gall[2, v] = total
        vec_start(2)

    @pl.loop(0, ncol // wide)
    def _(i):
        cols = pl.ds(pl.multiple_of(i * wide, wide), wide)
        householder = kbuf[:, slots:rows, cols].reshape(panel, wide)
        out_ref[:, cols] = out_ref[:, cols] - product(coeff, householder)

    @pl.when(r == 0)
    def _():
        vec_arrive(1)
        partial = product_t(secular_ref[...], gall[1].reshape(panel, panel))
        vec_arrive(2)
        correction = partial - product_t(coeff, gall[2].reshape(panel, panel))
        out_ref[:, 0:panel] = product_t(out_ref[:, 0:panel] - correction, pinv_ref[...])
        vec_sent(1)
        vec_sent(2)

    @pl.when(r != 0)
    def _():
        row_y_copy(r).wait_send()

    vec_sent(0)

    @pl.loop(1, nrow)
    def _(k):
        row_copy(k, r).wait_send()

    for phase in (0, 1):

        @pl.loop(0, zn)
        def _(zz):
            @pl.loop(0, yn)
            def _(yy):
                block = zz * yn + yy
                for sign in (-1, 1):
                    z_pass = (zz <= z if sign > 0 else zz >= z) & z_ok(sign)
                    y_pass = (yy <= y if sign > 0 else yy >= y) & y_ok(sign)

                    @pl.when(z_pass)
                    def _():
                        z_copy(phase, 1, block, sign).wait_send()

                    @pl.when(z_pass & (yy == y))
                    def _():
                        z_copy(phase, 0, block, sign).wait_send()

                    @pl.when(y_pass)
                    def _():
                        y_copy(phase, 0, block, sign).wait_send()

                    @pl.when(y_pass & (zz == z))
                    def _():
                        y_copy(phase, 1, block, sign).wait_send()


def per_device(
    nrow, nvec,
    old_vectors, panel_source, secular, reflectors, wy_factor, cholesky_panel, panel_inverse,
):
    panel = secular.shape[1]
    old_count, ncol = old_vectors.shape
    refl = reflectors.shape[0]
    yn = max(1, math.isqrt(nvec // 2))
    zn = nvec // yn
    slots = -(-(3 * (panel // nvec) // 2) // 8) * 8
    v = lax.axis_index("vec")
    r = lax.axis_index("row")
    owner = panel_source // old_count
    local = panel_source % old_count
    order = jnp.arange(panel, dtype=jnp.int32)
    before = (owner[:, None] == owner[None, :]) & (order[None, :] < order[:, None])
    earlier = jnp.sum(before.astype(jnp.int32), axis=1)
    slot_index = owner * slots + earlier
    mine = jnp.where(owner == v, earlier, -1)
    hit = mine[None, :] == jnp.arange(slots, dtype=jnp.int32)[:, None]
    source = jnp.sum(jnp.where(hit, local[None, :] + 1, 0), axis=1) - 1
    chooser = (source[:, None] == jnp.arange(old_count, dtype=jnp.int32)[None, :]).astype(
        jnp.float32
    )
    own = jnp.concatenate([product(chooser, old_vectors), reflectors], axis=0)
    below = r * ncol + jnp.arange(ncol, dtype=jnp.int32) >= panel
    masked = jnp.where(below[None, :], cholesky_panel, 0.0)
    rows = slots + refl
    vmem = pl.BlockSpec(memory_space=pltpu.VMEM)
    dma = pltpu.SemaphoreType.DMA
    return pl.pallas_call(
        functools.partial(kernel, nrow, zn, yn, slots),
        out_shape=jax.ShapeDtypeStruct((secular.shape[0], ncol), jnp.float32),
        in_specs=[vmem] * 6,
        out_specs=vmem,
        scratch_shapes=[
            pltpu.VMEM((nvec, rows, ncol), jnp.float32),
            pltpu.VMEM((2 * refl, panel), jnp.float32),
            pltpu.VMEM((refl, panel), jnp.float32),
            pltpu.VMEM((nrow, 2 * refl, panel), jnp.float32),
            pltpu.VMEM((nrow, refl, panel), jnp.float32),
            pltpu.VMEM((3, nvec, refl, panel), jnp.float32),
            pltpu.VMEM((secular.shape[0], nvec * slots), jnp.float32),
            dma,
            dma((2, 2, 4, nvec)),
            dma((2, 2, nvec)),
            dma((nrow,)),
            dma((nrow,)),
            dma,
            dma((nrow,)),
            dma((3, nvec)),
            dma((3, nvec)),
        ],
        compiler_params=pltpu.CompilerParams(
            collective_id=0, has_side_effects=True, vmem_limit_bytes=48 * 1024 * 1024
        ),
    )(own, masked, slot_index[None, :], secular, wy_factor, panel_inverse)


def solution(mesh):
    in_specs = (P("vec", "row"), P(), P("vec", None), P("vec", "row"), P(), P("vec", "row"), P())
    return jax.shard_map(
        functools.partial(per_device, mesh.shape["row"], mesh.shape["vec"]),
        mesh=mesh,
        in_specs=in_specs,
        out_specs=P("vec", "row"),
        check_vma=False,
    )
```

time: 118 us -> 110 us (0.932)
  Pallas kernels: 113 us -> 106 us
    pallas_call x1, Pallas kernels: 113 us -> 106 us  [per_device(): pl.pallas_call(functools.partial(kernel, nrow, zn, yn, slots), out_shape=...]
where the time goes in v2:
time: 110 us
  Pallas kernels  106 us (96%)
  other arithmetic  2.21 us (2%)
  local copies, waits for them, and re-layouts  1.56 us (1%)
    pallas_call x1, Pallas kernels, per_device(): pl.pallas_call(functools.partial(kernel, nrow, zn, yn, slots), out_shape=...  106 us

profile of v2, /device:TPU:0, one launch (start us, length us, event | category | flops | bytes accessed | tf_op | source)
XLA Modules:
  0.0 110.2 jit_solution(17437214075308932519)
XLA Ops:
  0.0 0.0 copy-start
  0.0 0.0 copy-start.4
  0.0 0.8 and_select_fusion.1
  0.8 0.2 convert_reduce_fusion
  1.0 0.1 select_reduce_fusion
  1.1 1.0 broadcast_select_fusion.chol_ref
  2.2 0.0 copy-done
  2.2 0.0 copy-start.1
  2.2 0.0 copy-start.2
  2.2 0.0 copy-start.3
  2.2 0.5 fusion.1
  2.8 0.0 copy-done.4
  2.8 0.1 pad_maximum_fusion.own_ref
  2.9 0.3 copy-done.1
  3.1 0.1 copy-done.2
  3.2 0.0 copy-done.3
  3.2 105.8 %shard_map.73 = f32[128,3072]{1,0:T(8,128)S(1)} custom-call(f32[80,3072]{1,0:T(8,128)S(1)} %pad_maximum_fusion.own_ref, f32[32,3072]{1,0:T(8,128)S(1)} %broadcast_select_fusion.chol_ref, s32[1,256]{1,0:T(1,128)S(1)} %bitcast.2, f32[128,256]{1,0:T(8,128)S(1)} %copy-done.3, f32[256,256]{1,0:T(8,128)S(1)} %copy-done.1, f32[256,256]{1,0:T(8,128)S(1)} %copy-done.2), custom_call_target="tpu_custom_call" | custom-call | tf_op jit(solution)/shard_map/pallas_call | solution.py:406
  109.1 1.1 %copy.9 = f32[128,3072]{1,0:T(8,128)} copy(f32[128,3072]{1,0:T(8,128)S(1)} %shard_map.73) | data formatting | bytes 3145728
  (3 shorter events, 0.0 us)
Async XLA Ops:
  0.0 2.2 %copy-start = (f32[80,3072]{1,0:T(8,128)S(1)}, f32[80,3072]{1,0:T(8,128)}, u32[]{:S(2)}) copy-start(f32[80,3072]{1,0:T(8,128)} %param.7) | copy-start | bytes 2949124
  0.0 2.8 %copy-start.4 = (f32[32,3072]{1,0:T(8,128)S(1)}, f32[32,3072]{1,0:T(8,128)}, u32[]{:S(2)}) copy-start(f32[32,3072]{1,0:T(8,128)} %param.10) | copy-start | bytes 1179652
  2.2 1.0 copy-start.1
  2.2 1.0 copy-start.2
  2.2 1.0 copy-start.3

commit v3 on v2

--- a/solution.py
+++ b/solution.py
@@ -146,7 +146,8 @@
 
                 @pl.when((zz >= 0) & (zz < zn))
                 def _():
-                    use(zz * yn + y)
+                    if use is not None:
+                        use(zz * yn + y)
 
             e = d - 1
             for side in (-1, 1):
@@ -164,52 +165,47 @@
                                 block = zz * yn + yy
                                 arrived(phase, 0, block)
                                 y_send(phase, 0, block, -sign)
-                                use(block)
+                                if use is not None:
+                                    use(block)
 
             hook(d)
 
     own_copy = pltpu.make_async_copy(own_ref, kbuf.at[v], own_sem)
     send_own(0)
     own_copy.start()
-    gram[...] = jnp.zeros_like(gram)
     gram_y[...] = jnp.zeros_like(gram_y)
     row_iota = lax.broadcasted_iota(jnp.int32, (nvec * slots, panel), 0)
     every = jnp.where(row_iota == slot_ref[0:1, :], 1.0, 0.0).astype(jnp.float32)
     smap[...] = product_t(secular_ref[...], every)
 
-    step = math.gcd(ncol, 768)
-
-    def add_picked(block):
-        def body(i, carry):
-            with_y, with_c = carry
-            cols = pl.ds(pl.multiple_of(i * step, step), step)
-            picked = kbuf[block, 0:slots, cols]
-            with_y = with_y + product_t(own_ref[slots:rows, cols], picked)
-            with_c = with_c + product_t(chol_ref[:, cols], picked)
-            return with_y, with_c
-
-        zero = jnp.zeros((refl, slots), jnp.float32)
-        with_y, with_c = lax.fori_loop(0, ncol // step, body, (zero, zero))
-        slot_iota = lax.broadcasted_iota(jnp.int32, (slots, panel), 0) + block * slots
-        chosen = jnp.where(slot_iota == slot_ref[0:1, :], 1.0, 0.0).astype(jnp.float32)
-        gram[0:refl] += product(with_y, chosen)
-        gram[refl : 2 * refl] += product(with_c, chosen)
-
-    def add_reflectors(block):
+    step = math.gcd(ncol, 1024)
+
+    def gram_picked():
         def body(i, carry):
             cols = pl.ds(pl.multiple_of(i * step, step), step)
-            return carry + product_t(chol_ref[:, cols], kbuf[block, slots:rows, cols])
-
-        y_with_c = lax.fori_loop(0, ncol // step, body, jnp.zeros((refl, refl), jnp.float32))
-        lane = lax.broadcasted_iota(jnp.int32, (refl, panel), 1)
-        sub = lax.broadcasted_iota(jnp.int32, (refl, panel), 0) + block * refl
-        placed = jnp.where(lane == sub, 1.0, 0.0).astype(jnp.float32)
-        gram_y[...] += product(y_with_c, placed)
+            picked = kbuf[:, 0:slots, cols].reshape(nvec * slots, step)
+            both = jnp.concatenate([own_ref[slots:rows, cols], chol_ref[:, cols]], axis=0)
+            return carry + product_t(both, picked)
+
+        zero = jnp.zeros((2 * refl, nvec * slots), jnp.float32)
+        sums = lax.fori_loop(0, ncol // step, body, zero)
+        slot_iota = lax.broadcasted_iota(jnp.int32, (nvec * slots, panel), 0)
+        chosen = jnp.where(slot_iota == slot_ref[0:1, :], 1.0, 0.0).astype(jnp.float32)
+        gram[...] = product(sums, chosen)
+
+    def place(sums, first):
+        lane = lax.broadcasted_iota(jnp.int32, (sums.shape[1], panel), 1)
+        sub = lax.broadcasted_iota(jnp.int32, (sums.shape[1], panel), 0) + first
+        gram_y[...] += product(sums, jnp.where(lane == sub, 1.0, 0.0).astype(jnp.float32))
+
+    def add_reflectors(block):
+        place(product_t(chol_ref[...], kbuf[block, slots:rows, :]), block * refl)
 
     own_copy.wait()
     relay_first(0)
-    add_picked(v)
-    relay(0, add_picked, lambda d: None)
+    relay(0, None, lambda d: None)
+    send_own(1)
+    gram_picked()
 
     def row_copy(k, slot):
         return pltpu.make_async_remote_copy(
@@ -271,7 +267,6 @@
     def _(k):
         row_copy(k, r).start()
 
-    send_own(1)
     rbuf[r] = gram[...]
     relay_first(1)
     add_reflectors(v)

time: 110 us -> 108 us (0.982)
  Pallas kernels: 106 us -> 103 us
    pallas_call x1, Pallas kernels: 106 us -> 103 us  [per_device(): pl.pallas_call(functools.partial(kernel, nrow, zn, yn, slots), out_shape=...]
where the time goes in v3:
time: 108 us; the launch traced here: 107 us
  Pallas kernels  103 us (95%)
  other arithmetic  2.21 us (2%)
  local copies, waits for them, and re-layouts  1.56 us (1%)
    pallas_call x1, Pallas kernels, per_device(): pl.pallas_call(functools.partial(kernel, nrow, zn, yn, slots), out_shape=...  103 us

profile of v3, /device:TPU:0, one launch (start us, length us, event | category | flops | bytes accessed | tf_op | source)
XLA Modules:
  0.0 107.5 jit_solution(3812514678016945049)
XLA Ops:
  0.0 0.0 copy-start
  0.0 0.0 copy-start.4
  0.0 0.8 and_select_fusion.1
  0.8 0.2 convert_reduce_fusion
  1.0 0.1 select_reduce_fusion
  1.1 1.0 broadcast_select_fusion.chol_ref
  2.2 0.0 copy-done
  2.2 0.0 copy-start.1
  2.2 0.0 copy-start.2
  2.2 0.0 copy-start.3
  2.2 0.5 fusion.1
  2.8 0.0 copy-done.4
  2.8 0.1 pad_maximum_fusion.own_ref
  2.9 0.3 copy-done.1
  3.1 0.1 copy-done.2
  3.2 0.0 copy-done.3
  3.2 103.1 %shard_map.73 = f32[128,3072]{1,0:T(8,128)S(1)} custom-call(f32[80,3072]{1,0:T(8,128)S(1)} %pad_maximum_fusion.own_ref, f32[32,3072]{1,0:T(8,128)S(1)} %broadcast_select_fusion.chol_ref, s32[1,256]{1,0:T(1,128)S(1)} %bitcast.2, f32[128,256]{1,0:T(8,128)S(1)} %copy-done.3, f32[256,256]{1,0:T(8,128)S(1)} %copy-done.1, f32[256,256]{1,0:T(8,128)S(1)} %copy-done.2), custom_call_target="tpu_custom_call" | custom-call | tf_op jit(solution)/shard_map/pallas_call | solution.py:401
  106.3 1.1 %copy.9 = f32[128,3072]{1,0:T(8,128)} copy(f32[128,3072]{1,0:T(8,128)S(1)} %shard_map.73) | data formatting | bytes 3145728
  (3 shorter events, 0.0 us)
Async XLA Ops:
  0.0 2.2 %copy-start = (f32[80,3072]{1,0:T(8,128)S(1)}, f32[80,3072]{1,0:T(8,128)}, u32[]{:S(2)}) copy-start(f32[80,3072]{1,0:T(8,128)} %param.7) | copy-start | bytes 2949124
  0.0 2.8 %copy-start.4 = (f32[32,3072]{1,0:T(8,128)S(1)}, f32[32,3072]{1,0:T(8,128)}, u32[]{:S(2)}) copy-start(f32[32,3072]{1,0:T(8,128)} %param.10) | copy-start | bytes 1179652
  2.2 1.0 copy-start.1
  2.2 1.0 copy-start.2
  2.2 1.0 copy-start.3
